TPU v7x, 256 devices: a whole 4x4x8 slice. The times are simulated.
256 devices in a mesh: dp: 8 (over z), expert: 32 (over y, x, core).
Axes of the slice: x: 4, y: 4, z: 8, core: 2. Of those that a mesh axis runs over, the one named last changes fastest.
Arguments:
- tokens: bfloat16 [32768, 2048], P(('dp', 'expert')), may hold values from -24 to 24
- expert_ids: int32 [32768, 2], P(('dp', 'expert')), may hold values from 0 to 31, as said below
- slot_index: int32 [32768, 2], P(('dp', 'expert')), may hold values from 0 to 15, as said below
- routing_gates: float32 [32768, 2], P(('dp', 'expert')), may hold values from 0.2 to 1
- grad_out: bfloat16 [32768, 2048], P(('dp', 'expert')), may hold values from -1.5 to 1.5
- w_gate: bfloat16 [32, 2048, 768], P('expert', 'dp'), may hold values from -0.125 to 0.125
- w_up: bfloat16 [32, 2048, 768], P('expert', 'dp'), may hold values from -0.125 to 0.125
- w_down: bfloat16 [32, 2048, 768], P('expert', 'dp'), may hold values from -0.21875 to 0.21875
Outputs:
- layer_out: bfloat16 [32768, 2048], P(('dp', 'expert'))
- grad_tokens: bfloat16 [32768, 2048], P(('dp', 'expert'))
- grad_gates: float32 [32768, 2], P(('dp', 'expert'))
- grad_w_gate: bfloat16 [32, 2048, 768], P('expert', 'dp')
- grad_w_up: bfloat16 [32, 2048, 768], P('expert', 'dp')
- grad_w_down: bfloat16 [32, 2048, 768], P('expert', 'dp')
Inputs may be any that keep to these rules, and one draw needn't show every extreme that they name: `expert_ids`: each row names 2 different experts. In each aligned block of 128 rows no expert is named more than 16 times; for each group of 32 blocks in a row, some expert is named exactly 16 times in every block of the group. `slot_index`: within one aligned block of 128 rows, the pairs that name one expert have distinct places, 0 up to their number minus one.
All inputs are finite; a program needn't handle non-finite values.
Results may differ from a plain program's by a relative error of at most 0.014.
Values may be sent and summed in bfloat16 or wider, within the bound.
A program may use at most 128 MiB of HBM per device.

v0:
```python
import jax
import jax.numpy as jnp
from jax import lax
from jax.sharding import PartitionSpec as P


def partial_term(left_rows, right_rows):
    return lax.dot_general(
        left_rows, right_rows, (((0,), (0,)), ((), ())), preferred_element_type=jnp.float32
    )


def on_device(tokens, expert_ids, slot_index, routing_gates, grad_out, w_gate, w_up, w_down):
    tok_dev, top_k = expert_ids.shape
    model_width = tokens.shape[1]
    experts = lax.axis_size("expert")
    capacity = 2 * tok_dev * top_k // experts
    target = (expert_ids * capacity + slot_index).reshape(-1)
    pair_index = jnp.arange(tok_dev * top_k, dtype=jnp.int32)
    source = jnp.full((experts * capacity,), -1, jnp.int32).at[target].set(pair_index)
    occupied = (source >= 0)[:, None]
    pair_safe = jnp.where(source >= 0, source, 0)
    token_safe = pair_safe // top_k
    zero_row = jnp.zeros((), jnp.bfloat16)
    outbound = jnp.where(occupied, tokens[token_safe], zero_row).reshape(
        experts, capacity, model_width
    )
    scaled = (routing_gates[:, :, None] * grad_out[:, None, :].astype(jnp.float32)).astype(
        jnp.bfloat16
    )
    scaled_rows = scaled.reshape(-1, model_width)
    grad_outbound = jnp.where(occupied, scaled_rows[pair_safe], zero_row).reshape(
        experts, capacity, model_width
    )
    gathered = (
        lax.all_gather(w_gate, "dp", axis=1, tiled=True),
        lax.all_gather(w_up, "dp", axis=1, tiled=True),
        lax.all_gather(w_down, "dp", axis=1, tiled=True),
    )
    full_gate = gathered[0][0]
    full_up = gathered[1][0]
    full_down = gathered[2][0]
    arrived = lax.all_to_all(outbound, "expert", split_axis=0, concat_axis=0, tiled=True)
    slot_count = arrived.shape[1]
    forward_flat_rows = arrived.reshape(-1, model_width)
    gate_pre = jnp.dot(forward_flat_rows, full_gate, preferred_element_type=jnp.float32)
    up_pre = jnp.dot(forward_flat_rows, full_up, preferred_element_type=jnp.float32)
    forward_hidden = (gate_pre * jax.nn.sigmoid(gate_pre) * up_pre).astype(jnp.bfloat16)
    produced = jnp.dot(forward_hidden, full_down.T, preferred_element_type=jnp.float32).astype(
        jnp.bfloat16
    )
    returned = lax.all_to_all(
        produced.reshape(experts, slot_count, model_width),
        "expert",
        split_axis=0,
        concat_axis=0,
        tiled=True,
    )
    returned, arrived, gate_stack, up_stack = (
        returned,
        arrived,
        gate_pre.reshape(experts, slot_count, -1),
        up_pre.reshape(experts, slot_count, -1),
    )
    grad_arrived = lax.all_to_all(grad_outbound, "expert", split_axis=0, concat_axis=0, tiled=True)
    by_pair = returned.reshape(-1, model_width)[target].reshape(tok_dev, top_k, model_width)
    layer_out = jnp.sum(by_pair.astype(jnp.float32) * routing_gates[:, :, None], axis=1).astype(
        jnp.bfloat16
    )
    grad_gates = jnp.einsum("tkd,td->tk", by_pair, grad_out, preferred_element_type=jnp.float32)
    flat_grad = grad_arrived.reshape(-1, model_width)
    flat_rows = arrived.reshape(-1, model_width)
    gate_flat = gate_stack.reshape(flat_grad.shape[0], -1)
    up_flat = up_stack.reshape(flat_grad.shape[0], -1)
    sigmoid_gate = jax.nn.sigmoid(gate_flat)
    active = gate_flat * sigmoid_gate
    hidden = (active * up_flat).astype(jnp.bfloat16)
    down_back = jnp.dot(flat_grad, full_down, preferred_element_type=jnp.float32)
    silu_slope = sigmoid_gate * (1.0 + gate_flat * (1.0 - sigmoid_gate))
    grad_gate_pre = (down_back * up_flat * silu_slope).astype(jnp.bfloat16)
    grad_up_pre = (down_back * active).astype(jnp.bfloat16)
    input_back = (
        jnp.dot(grad_gate_pre, full_gate.T, preferred_element_type=jnp.float32)
        + jnp.dot(grad_up_pre, full_up.T, preferred_element_type=jnp.float32)
    ).astype(jnp.bfloat16)
    input_return = lax.all_to_all(
        input_back.reshape(experts, capacity, model_width),
        "expert",
        split_axis=0,
        concat_axis=0,
        tiled=True,
    )
    back_pairs = input_return.reshape(-1, model_width)[target].reshape(tok_dev, top_k, model_width)
    grad_tokens = jnp.sum(back_pairs.astype(jnp.float32), axis=1).astype(jnp.bfloat16)
    grad_gate_w = lax.psum_scatter(
        partial_term(flat_rows, grad_gate_pre).astype(jnp.bfloat16),
        "dp",
        scatter_dimension=0,
        tiled=True,
    )
    grad_up_w = lax.psum_scatter(
        partial_term(flat_rows, grad_up_pre).astype(jnp.bfloat16),
        "dp",
        scatter_dimension=0,
        tiled=True,
    )
    grad_down_w = lax.psum_scatter(
        partial_term(flat_grad, hidden).astype(jnp.bfloat16), "dp", scatter_dimension=0, tiled=True
    )
    return (
        layer_out,
        grad_tokens,
        grad_gates,
        grad_gate_w[None],
        grad_up_w[None],
        grad_down_w[None],
    )


def solution(mesh):
    in_specs = (
        P(("dp", "expert"), None),
        P(("dp", "expert"), None),
        P(("dp", "expert"), None),
        P(("dp", "expert"), None),
        P(("dp", "expert"), None),
        P("expert", "dp", None),
        P("expert", "dp", None),
        P("expert", "dp", None),
    )
    out_specs = (
        P(("dp", "expert"), None),
        P(("dp", "expert"), None),
        P(("dp", "expert"), None),
        P("expert", "dp", None),
        P("expert", "dp", None),
        P("expert", "dp", None),
    )
    return jax.shard_map(
        on_device, mesh=mesh, in_specs=in_specs, out_specs=out_specs, check_vma=False
    )
```

profile of v0, /device:TPU:2, one launch (start us, length us, event | category | flops | bytes accessed | tf_op | source)
XLA Modules:
  0.0 312.3 jit_solution(7386118729877439063)
XLA Ops:
  17.9 3.3 %gather_fusion.2 = bf16[512,2048]{1,0:T(8,128)(2,1)} fusion(bf16[256,2048]{1,0:T(8,128)(2,1)S(1)} %multiply_convert_fusion, s32[1024]{0:T(1024)S(1)} %get-tuple-element.13), kind=kCustom, calls=%fused_computation.2 | custom fusion | bytes 4196352 | tf_op jit(solution)/shard_map/gather | solution.py:32
  21.2 3.3 %gather_fusion = bf16[512,2048]{1,0:T(8,128)(2,1)} fusion(bf16[128,2048]{1,0:T(8,128)(2,1)S(1)} %copy-done, s32[1024]{0:T(1024)S(1)} %get-tuple-element.14), kind=kCustom, calls=%fused_computation | custom fusion | bytes 4196352 | tf_op jit(solution)/shard_map/gather | solution.py:25
  24.5 3.2 %broadcast_select_fusion = (bf16[32,16,2048]{2,1,0:T(8,128)(2,1)S(1)}, bf16[32,16,2048]{2,1,0:T(8,128)(2,1)}) fusion(bf16[32,16,2048]{2,1,0:T(8,128)(2,1)S(1)} %bitcast.49, pred[32,16]{1,0:T(8,128)(4,1)S(1)} %broadcast_in_dim.46, bf16[32,16,2048]{2,1,0:T(8,128)(2,1)} %bitcast.50), kind=kLoop, calls=%fused_computation.24 | loop fusion | flops 2097152 | bytes 8389120 | tf_op jit(solution)/shard_map/jit(_where)/select_n | solution.py:32
  27.7 34.6 %all_to_all.20 = bf16[32,16,2048]{2,1,0:T(8,128)(2,1)S(1)} all-to-all(bf16[32,16,2048]{2,1,0:T(8,128)(2,1)S(1)} %get-tuple-element.9), channel_id=1, replica_groups=mesh['dp'=8,'expert'=32] {'expert'}, dimensions={0} | all-to-all | bytes 4194304 | tf_op jit(solution)/shard_map/all_to_all | solution.py:65
  62.4 5.8 %all-to-all-start = ((bf16[32,16,2048]{2,1,0:T(8,128)(2,1)}), bf16[32,16,2048]{2,1,0:T(8,128)(2,1)}, u32[]{:S(2)}, u32[]{:S(2)}) async-start(bf16[32,16,2048]{2,1,0:T(8,128)(2,1)} %get-tuple-element.10), calls=%async_computation | async-start | bytes 4194304 | tf_op jit(solution)/shard_map/all_to_all | solution.py:43
  68.4 5.1 %fusion = f32[512,768]{1,0:T(8,128)} fusion(bf16[512,2048]{1,0:T(8,128)(2,1)S(1)} %bitcast.51, bf16[1,2048,768]{2,1,0:T(8,128)(2,1)} %all-gather.8.cloned.1.call-done), kind=kOutput, calls=%fused_computation.9 | convolution fusion | flops 1610612736 | bytes 6815744 | tf_op jit(solution)/shard_map/dot_general | solution.py:78
  73.5 22.8 %all-to-all-done = bf16[32,16,2048]{2,1,0:T(8,128)(2,1)} async-done(((bf16[32,16,2048]{2,1,0:T(8,128)(2,1)}), bf16[32,16,2048]{2,1,0:T(8,128)(2,1)}, u32[]{:S(2)}, u32[]{:S(2)}) %all-to-all-start) | async-done | bytes 2097184 | tf_op jit(solution)/shard_map/all_to_all | solution.py:43
  96.3 6.9 %all-gather.6.cloned.1.call-done = bf16[1,2048,768]{2,1,0:T(8,128)(2,1)} async-done(((bf16[1,256,768]{2,1,0:T(8,128)(2,1)}), bf16[1,2048,768]{2,1,0:T(8,128)(2,1)}) %all-gather.6.cloned.1.call-update) | async-done | bytes 3145744 | tf_op jit(solution)/shard_map/all_gather | solution.py:37
  103.2 5.4 %fusion.6 = f32[512,768]{1,0:T(8,128)} fusion(bf16[512,2048]{1,0:T(8,128)(2,1)} %bitcast.2, bf16[1,2048,768]{2,1,0:T(8,128)(2,1)} %all-gather.6.cloned.1.call-done), kind=kOutput, calls=%fused_computation.15 | convolution fusion | flops 1610612736 | bytes 6815744 | tf_op jit(solution)/shard_map/dot_general | solution.py:47
  108.6 40.0 %all-gather.4.cloned.1.call-done = bf16[1,2048,768]{2,1,0:T(8,128)(2,1)} async-done(((bf16[1,256,768]{2,1,0:T(8,128)(2,1)}), bf16[1,2048,768]{2,1,0:T(8,128)(2,1)}) %all-gather.4.cloned.1.call-update) | async-done | bytes 3145744 | tf_op jit(solution)/shard_map/all_gather | solution.py:36
  148.6 6.9 %multiply_convert_fusion.2 = (bf16[512,768]{1,0:T(8,128)(2,1)S(1)}, bf16[512,768]{1,0:T(8,128)(2,1)}, bf16[512,768]{1,0:T(8,128)(2,1)}) fusion(f32[512,768]{1,0:T(8,128)} %fusion, f32[512,768]{1,0:T(8,128)} %fusion.6, bf16[512,2048]{1,0:T(8,128)(2,1)} %bitcast.2, bf16[1,2048,768]{2,1,0:T(8,128)(2,1)} %all-gather.4.cloned.1.call-done), kind=kOutput, calls=%fused_computation.27 | convolution fusion | flops 1616510976 | bytes 10747904 | tf_op jit(solution)/shard_map/dot_general | solution.py:46
  155.5 5.1 %convolution_convert_fusion.2 = bf16[2048,768]{1,0:T(8,128)(2,1)} fusion(bf16[512,2048]{1,0:T(8,128)(2,1)} %bitcast.2, bf16[512,768]{1,0:T(8,128)(2,1)S(1)} %get-tuple-element.6), kind=kOutput, calls=%fused_computation.8 | convolution fusion | flops 1612185600 | bytes 6029312 | tf_op jit(solution)/shard_map/dot_general | solution.py:8
  160.7 5.2 %convolution_convert_fusion.1 = bf16[2048,768]{1,0:T(8,128)(2,1)} fusion(bf16[512,2048]{1,0:T(8,128)(2,1)} %bitcast.2, bf16[512,768]{1,0:T(8,128)(2,1)} %get-tuple-element.7), kind=kOutput, calls=%fused_computation.7 | convolution fusion | flops 1612185600 | bytes 6029312 | tf_op jit(solution)/shard_map/dot_general | solution.py:8
  166.0 4.6 %convolution_convert_fusion = bf16[2048,768]{1,0:T(8,128)(2,1)} fusion(bf16[512,2048]{1,0:T(8,128)(2,1)S(1)} %bitcast.52, bf16[512,768]{1,0:T(8,128)(2,1)} %get-tuple-element.8), kind=kOutput, calls=%fused_computation.6 | convolution fusion | flops 1612185600 | bytes 6029312 | tf_op jit(solution)/shard_map/dot_general | solution.py:8
  171.8 5.0 %fusion.12 = bf16[512,2048]{1,0:T(8,128)(2,1)} fusion(bf16[512,768]{1,0:T(8,128)(2,1)S(1)} %copy-done.8, bf16[1,2048,768]{2,1,0:T(8,128)(2,1)} %all-gather.8.cloned.1.call-done), kind=kOutput, calls=%fused_computation.21 | convolution fusion | flops 1611661312 | bytes 6029312 | tf_op jit(solution)/shard_map/dot_general | solution.py:49
  176.8 7.4 %all-to-all-start.1 = ((bf16[32,16,2048]{2,1,0:T(8,128)(2,1)}), bf16[32,16,2048]{2,1,0:T(8,128)(2,1)S(1)}, u32[]{:S(2)}, u32[]{:S(2)}) async-start(bf16[32,16,2048]{2,1,0:T(8,128)(2,1)} %bitcast.54), calls=%async_computation.1 | async-start | bytes 4194304 | tf_op jit(solution)/shard_map/all_to_all | solution.py:52
  184.3 4.1 %fusion.4 = f32[512,2048]{1,0:T(8,128)S(1)} fusion(bf16[512,768]{1,0:T(8,128)(2,1)} %get-tuple-element.7, bf16[1,2048,768]{2,1,0:T(8,128)(2,1)} %all-gather.6.cloned.1.call-done), kind=kOutput, calls=%fused_computation.13 | convolution fusion | flops 1610612736 | bytes 8126464 | tf_op jit(solution)/shard_map/dot_general | solution.py:84
  191.6 20.6 %all-to-all-done.1 = bf16[32,16,2048]{2,1,0:T(8,128)(2,1)S(1)} async-done(((bf16[32,16,2048]{2,1,0:T(8,128)(2,1)}), bf16[32,16,2048]{2,1,0:T(8,128)(2,1)S(1)}, u32[]{:S(2)}, u32[]{:S(2)}) %all-to-all-start.1) | async-done | bytes 2097184 | tf_op jit(solution)/shard_map/all_to_all | solution.py:52
  212.2 6.7 %all-to-all-start.3 = ((bf16[32,16,2048]{2,1,0:T(8,128)(2,1)}), bf16[32,16,2048]{2,1,0:T(8,128)(2,1)}, u32[]{:S(2)}, u32[]{:S(2)}) async-start(bf16[32,16,2048]{2,1,0:T(8,128)(2,1)} %bitcast.53), calls=%async_computation.3 | async-start | bytes 4194304 | tf_op jit(solution)/shard_map/all_to_all | solution.py:86
  223.0 24.0 %all-to-all-done.3 = bf16[32,16,2048]{2,1,0:T(8,128)(2,1)} async-done(((bf16[32,16,2048]{2,1,0:T(8,128)(2,1)}), bf16[32,16,2048]{2,1,0:T(8,128)(2,1)}, u32[]{:S(2)}, u32[]{:S(2)}) %all-to-all-start.3) | async-done | bytes 2097184 | tf_op jit(solution)/shard_map/all_to_all | solution.py:86
  247.0 4.2 %gather_fusion.3 = bf16[256,2048]{1,0:T(8,128)(2,1)S(1)} fusion(bf16[512,2048]{1,0:T(8,128)(2,1)} %bitcast.11, s32[1024]{0:T(1024)S(1)} %pad_clamp_fusion.1), kind=kCustom, calls=%fused_computation.3 | custom fusion | bytes 2098176 | tf_op jit(solution)/shard_map/gather | solution.py:93
  255.8 3.6 %reduce_sum.22 = bf16[128,2048]{1,0:T(8,128)(2,1)} reduce(bf16[128,2,2048]{2,1,0:T(2,128)(2,1)S(1)} %copy-done.2, bf16[]{:T(256)} %constant.29.clone.1), dimensions={1}, to_apply=%region_2.3 | reduce | flops 262144 | bytes 1572866 | tf_op jit(solution)/shard_map/reduce_sum | solution.py:94
  259.4 3.9 %multiply_reduce_fusion = bf16[128,2048]{1,0:T(8,128)(2,1)} fusion(bf16[128,2,2048]{2,1,0:T(2,128)(2,1)S(1)} %reshape.92, f32[128,2]{1,0:T(8,128)S(1)} %copy.16), kind=kLoop, calls=%fused_computation.23 | loop fusion | flops 1310720 | bytes 1573888 | tf_op jit(solution)/shard_map/reduce_sum | solution.py:67
  263.3 42.2 %reduce-scatter.8.cloned.1.call-done = bf16[256,768]{1,0:T(8,128)(2,1)} async-done(((bf16[2048,768]{1,0:T(8,128)(2,1)}), bf16[256,768]{1,0:T(8,128)(2,1)}) %reduce-scatter.8.cloned.1.call-update) | async-done | bytes 393232 | tf_op jit(solution)/shard_map/reduce_scatter | solution.py:107
  (55 shorter events, 23.8 us)
Async XLA Ops:
  7.2 14.0 %copy-start = (bf16[128,2048]{1,0:T(8,128)(2,1)S(1)}, bf16[128,2048]{1,0:T(8,128)(2,1)}, u32[]{:S(2)}) copy-start(bf16[128,2048]{1,0:T(8,128)(2,1)} %param.8) | copy-start | bytes 1572868
  7.2 61.3 %all-gather.8.cloned.1.call-start = ((), (), s32[]{:S(2)}) async-start(), calls=%async_computation.9 | async-start | bytes 3538944 | tf_op jit(solution)/shard_map/all_gather | solution.py:38
  7.9 95.3 %all-gather.6.cloned.1.call-start = ((), (), s32[]{:S(2)}) async-start(), calls=%async_computation.8 | async-start | bytes 3538944 | tf_op jit(solution)/shard_map/all_gather | solution.py:37
  8.7 140.0 %all-gather.4.cloned.1.call-start = ((), (), s32[]{:S(2)}) async-start(), calls=%async_computation.7 | async-start | bytes 3538944 | tf_op jit(solution)/shard_map/all_gather | solution.py:36
  11.5 2.5 copy-start.4
  11.5 2.7 copy-start.5
  11.5 2.7 copy-start.6
  21.2 3.3 %copy-start.1 = (bf16[512,2048]{1,0:T(8,128)(2,1)S(1)}, bf16[512,2048]{1,0:T(8,128)(2,1)}, u32[]{:S(2)}) copy-start(bf16[512,2048]{1,0:T(8,128)(2,1)} %gather_fusion.2) | copy-start | bytes 6291460
  62.4 33.9 %all-to-all-start = ((bf16[32,16,2048]{2,1,0:T(8,128)(2,1)}), bf16[32,16,2048]{2,1,0:T(8,128)(2,1)}, u32[]{:S(2)}, u32[]{:S(2)}) async-start(bf16[32,16,2048]{2,1,0:T(8,128)(2,1)} %get-tuple-element.10), calls=%async_computation | async-start | bytes 4194304 | tf_op jit(solution)/shard_map/all_to_all | solution.py:43
  68.2 195.1 %reduce-scatter.4.cloned.1.call-start = ((), (), s32[]{:S(2)}) async-start(), calls=%async_computation.10 | async-start | bytes 3538944 | tf_op jit(solution)/shard_map/reduce_scatter | solution.py:95
  160.7 102.6 %reduce-scatter.6.cloned.1.call-start = ((), (), s32[]{:S(2)}) async-start(), calls=%async_computation.11 | async-start | bytes 3538944 | tf_op jit(solution)/shard_map/reduce_scatter | solution.py:101
  166.0 139.5 %reduce-scatter.8.cloned.1.call-start = ((), (), s32[]{:S(2)}) async-start(), calls=%async_computation.12 | async-start | bytes 3538944 | tf_op jit(solution)/shard_map/reduce_scatter | solution.py:107
  170.7 1.2 copy-start.8
  176.8 35.3 %all-to-all-start.1 = ((bf16[32,16,2048]{2,1,0:T(8,128)(2,1)}), bf16[32,16,2048]{2,1,0:T(8,128)(2,1)S(1)}, u32[]{:S(2)}, u32[]{:S(2)}) async-start(bf16[32,16,2048]{2,1,0:T(8,128)(2,1)} %bitcast.54), calls=%async_computation.1 | async-start | bytes 4194304 | tf_op jit(solution)/shard_map/all_to_all | solution.py:52
  184.3 4.1 %copy-start.7 = (bf16[1,2048,768]{2,1,0:T(8,128)(2,1)S(1)}, bf16[1,2048,768]{2,1,0:T(8,128)(2,1)}, u32[]{:S(2)}) copy-start(bf16[1,2048,768]{2,1,0:T(8,128)(2,1)} %all-gather.4.cloned.1.call-done) | copy-start | bytes 9437188
  212.2 34.8 %all-to-all-start.3 = ((bf16[32,16,2048]{2,1,0:T(8,128)(2,1)}), bf16[32,16,2048]{2,1,0:T(8,128)(2,1)}, u32[]{:S(2)}, u32[]{:S(2)}) async-start(bf16[32,16,2048]{2,1,0:T(8,128)(2,1)} %bitcast.53), calls=%async_computation.3 | async-start | bytes 4194304 | tf_op jit(solution)/shard_map/all_to_all | solution.py:86
  251.3 1.5 copy-start.3
  252.8 3.0 copy-start.2
Sparse Core Ops, SparseCore 0:
  9.8 47.9 all-gather.7
  59.5 43.6 all-gather.5
  105.0 43.5 all-gather.3
  160.8 45.7 reduce-scatter.3
  209.5 46.2 reduce-scatter.5
  258.8 46.5 reduce-scatter.7
where the time goes:
time: 313 us; the launch traced here: 312 us
  waiting for transfers between devices  159 us (51%)
  matrix products  47 us (15%)
  blocking collectives  34.6 us (11%)
  local copies, waits for them, and re-layouts  24.8 us (8%)
  starting transfers between devices  20.4 us (7%)
  between operations  14.3 us (5%)
  other arithmetic  12.5 us (4%)
    reduce_scatter x1, waiting for transfers between devices, on_device(): lax.psum_scatter(partial_term(flat_grad, hidden).astype(jnp.bfloat16), 'd...  42.2 us
    all_gather x1, waiting for transfers between devices, on_device(): lax.all_gather(w_gate, 'dp', axis=1, tiled=True)  40 us
    all_to_all x1, blocking collectives, on_device(): lax.all_to_all(grad_outbound, 'expert', split_axis=0, concat_axis=0, tile...  34.6 us
    all_to_all x1, waiting for transfers between devices, on_device(): lax.all_to_all(input_back.reshape(experts, capacity, model_width), 'exper...  24 us
    all_to_all x1, waiting for transfers between devices, on_device(): lax.all_to_all(outbound, 'expert', split_axis=0, concat_axis=0, tiled=True)  22.8 us
    all_to_all x1, waiting for transfers between devices, on_device(): lax.all_to_all(produced.reshape(experts, slot_count, model_width), 'exper...  20.6 us
    dot_general x3, matrix products, partial_term(): lax.dot_general(left_rows, right_rows, (((0,), (0,)), ((), ())), preferre...  15 us
    all_to_all x1, starting transfers between devices, on_device(): lax.all_to_all(produced.reshape(experts, slot_count, model_width), 'exper...  7.43 us
  transfers between devices with their start and end apart: 9, of which 6 were waited for; matrix products, arithmetic and copies ran while one was open for 23% of the time, Pallas kernels for 0%

commit v1 on v0

v1 whole, which is shorter than its diff:
```python
import functools

import jax
import jax.numpy as jnp
from jax import lax
from jax.experimental import pallas as pl
from jax.experimental.pallas import tpu as pltpu
from jax.sharding import PartitionSpec as P

MESH = pl.DeviceIdType.MESH
F32 = jnp.float32
BF16 = jnp.bfloat16
GATE, UP, DOWN = 0, 1, 2
WIDE = 256


def layer_kernel(
    nz, ne, nx, nc, cap,
    tgt_l, gate_l, tgt_s, gate_s, tok, gout, wg, wu, wd,
    lo, gt, gg, og, ou, od,
    wfull, outx, outg, arrx, arrg, pre, act, prod, back, ret, retb, xt, rsr, rss, onehot, slot_gate,
    own_sem, ag_send, ag_recv, rs_send, rs_recv, a2a_send, a2a_recv,
):
    z = lax.axis_index("dp")
    me = lax.axis_index("expert")
    right, left = lax.rem(z + 1, nz), lax.rem(z + nz - 1, nz)
    peers = (right, left)
    width = tok.shape[1]
    hidden_units = wg.shape[2]
    shard = wg.shape[1]
    half = shard // 2
    rows = outx.shape[0]
    last = nz - 2

    own = pl.ds(pl.multiple_of(z * shard, shard), shard)
    own_copies = [
        pltpu.make_async_copy(ref.at[0], wfull.at[w, own, :], own_sem.at[w])
        for w, ref in ((GATE, wg), (UP, wu), (DOWN, wd))
    ]
    for copy in own_copies:
        copy.start()

    def partner(o, sign):
        oc, ox, oy = lax.rem(o, nc), lax.rem(o // nc, nx), o // (nc * nx)
        c, x, y = lax.rem(me, nc), lax.rem(me // nc, nx), me // (nc * nx)
        ny = ne // (nc * nx)
        c = lax.rem(c + sign * oc + nc, nc)
        x = lax.rem(x + sign * ox + nx, nx)
        y = lax.rem(y + sign * oy + ny, ny)
        return (y * nx + x) * nc + c

    barrier = pltpu.get_barrier_semaphore()
    for peer in peers:
        pl.semaphore_signal(barrier, inc=1, device_id={"dp": peer}, device_id_type=MESH)

    @pl.loop(1, ne)
    def _(o):
        pl.semaphore_signal(barrier, inc=1, device_id={"expert": partner(o, 1)}, device_id_type=MESH)

    slot = lax.broadcasted_iota(jnp.int32, onehot.shape, 0)
    hit0, hit1 = slot == tgt_l[0:1, :], slot == tgt_l[1:2, :]
    onehot[...] = jnp.where(hit0 | hit1, 1.0, 0.0).astype(BF16)
    gates = jnp.where(hit0, gate_l[0:1, :], 0.0) + jnp.where(hit1, gate_l[1:2, :], 0.0)
    slot_gate[...] = jnp.broadcast_to(jnp.sum(gates, axis=1, keepdims=True), slot_gate.shape)

    def columns(n, size=WIDE):
        return pl.ds(pl.multiple_of(n * size, size), size)

    def block(e):
        return pl.ds(pl.multiple_of(e * cap, cap), cap)

    @pl.loop(0, width // WIDE)
    def _(n):
        cols = columns(n)
        outx[:, cols] = jnp.dot(onehot[...], tok[:, cols], preferred_element_type=F32).astype(BF16)

    def piece(w, src, h):
        start = pl.multiple_of(lax.rem(src + 2 * nz, nz) * shard + h * half, half)
        return wfull.at[w, pl.ds(start, half), :]

    def gather_copy(w, h, s, arriving=False):
        hop = s + 1 if arriving else s
        ref = piece(w, z - hop if h == 0 else z + hop, h)
        return pltpu.make_async_remote_copy(
            src_ref=ref, dst_ref=ref,
            send_sem=ag_send.at[w, h, s], recv_sem=ag_recv.at[w, h, s],
            device_id={"dp": peers[h]}, device_id_type=MESH,
        )

    def exchange(src, dst, k, o, arriving=False):
        dest = partner(o, 1)
        landing = partner(o, -1) if arriving else me
        return pltpu.make_async_remote_copy(
            src_ref=src.at[block(dest), :], dst_ref=dst.at[block(landing), :],
            send_sem=a2a_send.at[k, o], recv_sem=a2a_recv.at[k, o],
            device_id={"expert": dest}, device_id_type=MESH,
        )

    def send_rows(src, dst, k):
        @pl.loop(1, ne)
        def _(o):
            exchange(src, dst, k, o).start()

        mine = block(me)
        dst[mine, :] = src[mine, :]

    def await_rows(src, dst, k):
        @pl.loop(1, ne)
        def _(o):
            exchange(src, dst, k, o, arriving=True).wait_recv()

    for copy in own_copies:
        copy.wait()
    pl.semaphore_wait(barrier, ne + 1)
    for w in (GATE, UP, DOWN):
        for h in (0, 1):
            gather_copy(w, h, 0).start()
    send_rows(outx, arrx, 0)

    @pl.loop(0, width // WIDE)
    def _(n):
        cols = columns(n)
        picked = jnp.dot(onehot[...], gout[:, cols], preferred_element_type=F32)
        outg[:, cols] = (picked * slot_gate[:, 0:1]).astype(BF16)

    pre[...] = jnp.zeros_like(pre)
    send_rows(outg, arrg, 1)

    def halves(j):
        a = pl.multiple_of(lax.rem(z - j + 2 * nz, nz) * shard, half)
        b = pl.multiple_of(lax.rem(z + j, nz) * shard + half, half)
        return pl.ds(a, half), pl.ds(b, half)

    def accumulate(w, lhs_ref, j):
        a, b = halves(j)
        lhs = jnp.concatenate([lhs_ref[:, a], lhs_ref[:, b]], axis=1)
        for n in range(hidden_units // WIDE):
            cols = slice(n * WIDE, (n + 1) * WIDE)
            rhs = jnp.concatenate([wfull[w, a, cols], wfull[w, b, cols]], axis=0)
            pre[w, :, cols] += jnp.dot(lhs, rhs, preferred_element_type=F32)

    def accumulate_gate_up(lo_j, hi_j):
        @pl.loop(lo_j, hi_j)
        def _(j):
            @pl.loop(0, 2)
            def _(w):
                accumulate(w, arrx, j)

    def accumulate_down(lo_j, hi_j):
        @pl.loop(lo_j, hi_j)
        def _(j):
            accumulate(DOWN, arrg, j)

    def transpose(k, src):
        @pl.loop(0, width // WIDE)
        def _(n):
            cols = columns(n)
            xt[k, cols, :] = src[:, cols].T

    x_step, g_step = min(3, last - 1), min(5, last - 1)

    @pl.loop(0, last)
    def _(s):
        for w in (GATE, UP, DOWN):
            for h in (0, 1):
                gather_copy(w, h, s, arriving=True).wait_recv()
                gather_copy(w, h, s + 1).start()

        @pl.when(s == x_step)
        def _():
            await_rows(outx, arrx, 0)

        @pl.when(s >= x_step)
        def _():
            accumulate_gate_up(jnp.where(s == x_step, 0, s + 1), s + 2)

        @pl.when(s == x_step)
        def _():
            transpose(0, arrx)

        @pl.when(s == g_step)
        def _():
            await_rows(outg, arrg, 1)
            accumulate_down(0, s + 2)
            transpose(1, arrg)

        @pl.when(s > g_step)
        def _():
            accumulate_down(s + 1, s + 2)

    tile = 64

    def gating(rows_now):
        g = pre[GATE, rows_now, :]
        sig = jax.nn.sigmoid(g)
        return g, pre[UP, rows_now, :], sig, g * sig

    def scatter_copy(w, h, i):
        part = pl.ds(h * half, half)
        return pltpu.make_async_remote_copy(
            src_ref=rss.at[w, i - 1, part, :], dst_ref=rsr.at[w, i - 1, part, :],
            send_sem=rs_send.at[w, h, i - 1], recv_sem=rs_recv.at[w, h, i - 1],
            device_id={"dp": peers[h]}, device_id_type=MESH,
        )

    def scatter_step(w, i, first=False, out=None):
        a, b = halves(i)
        if not first:
            for h in (0, 1):
                scatter_copy(w, h, i - 1).wait_recv()
        k = w // 2
        lhs = jnp.concatenate([xt[k, a, :], xt[k, b, :]], axis=0)
        for n in range(hidden_units // WIDE):
            cols = slice(n * WIDE, (n + 1) * WIDE)
            term = jnp.dot(lhs, act[w, :, cols], preferred_element_type=F32)
            if not first:
                term = term + rsr[w, i - 2, :, cols].astype(F32)
            if out is None:
                rss[w, i - 1, :, cols] = term.astype(BF16)
            else:
                out[0, :, cols] = term.astype(BF16)
        if out is None:
            for h in (0, 1):
                scatter_copy(w, h, i).start()

    for h in (0, 1):
        gather_copy(GATE, h, last, arriving=True).wait_recv()
    for h in (0, 1):
        gather_copy(UP, h, last, arriving=True).wait_recv()
    accumulate_gate_up(nz - 1, nz)

    @pl.loop(0, rows // tile)
    def _(r):
        rows_now = pl.ds(pl.multiple_of(r * tile, tile), tile)
        _, u, _, active = gating(rows_now)
        act[DOWN, rows_now, :] = (active * u).astype(BF16)

    scatter_step(DOWN, 1, first=True)
    for h in (0, 1):
        gather_copy(DOWN, h, last, arriving=True).wait_recv()
    accumulate_down(nz - 1, nz)

    @pl.loop(0, rows // tile)
    def _(r):
        rows_now = pl.ds(pl.multiple_of(r * tile, tile), tile)
        g, u, sig, active = gating(rows_now)
        d = pre[DOWN, rows_now, :]
        slope = sig * (1.0 + g * (1.0 - sig))
        act[GATE, rows_now, :] = (d * u * slope).astype(BF16)
        act[UP, rows_now, :] = (d * active).astype(BF16)

    @pl.loop(0, 2)
    def _(w):
        scatter_step(w, 1, first=True)

    def times_transposed(left, w, n):
        return lax.dot_general(
            left, wfull[w, columns(n), :], (((1,), (1,)), ((), ())), preferred_element_type=F32
        )

    @pl.loop(0, width // WIDE)
    def _(n):
        prod[:, columns(n)] = times_transposed(act[DOWN], DOWN, n).astype(BF16)

    send_rows(prod, ret, 2)

    def input_back():
        @pl.loop(0, width // WIDE)
        def _(n):
            total = times_transposed(act[GATE], GATE, n) + times_transposed(act[UP], UP, n)
            back[:, columns(n)] = total.astype(BF16)

        send_rows(back, retb, 3)

    tok_dev = tok.shape[0]
    slots = lax.broadcasted_iota(jnp.int32, (tok_dev, rows), 1)

    def picks():
        return (
            jnp.where(slots == tgt_s[:, 0:1], 1.0, 0.0).astype(BF16),
            jnp.where(slots == tgt_s[:, 1:2], 1.0, 0.0).astype(BF16),
        )

    def combine_out():
        await_rows(prod, ret, 2)
        pick0, pick1 = picks()
        zero = jnp.zeros((tok_dev, 1), F32)

        def step(n, sums):
            cols = columns(n)
            r0 = jnp.dot(pick0, ret[:, cols], preferred_element_type=F32)
            r1 = jnp.dot(pick1, ret[:, cols], preferred_element_type=F32)
            lo[:, cols] = (gate_s[:, 0:1] * r0 + gate_s[:, 1:2] * r1).astype(BF16)
            cot = gout[:, cols].astype(F32)
            return (
                sums[0] + jnp.sum(r0 * cot, axis=1, keepdims=True),
                sums[1] + jnp.sum(r1 * cot, axis=1, keepdims=True),
            )

        d0, d1 = lax.fori_loop(0, width // WIDE, step, (zero, zero))
        which = lax.broadcasted_iota(jnp.int32, gg.shape, 1)
        gg[...] = jnp.where(which == 0, d0, d1)

    def combine_back():
        await_rows(back, retb, 3)
        pick0, pick1 = picks()

        @pl.loop(0, width // WIDE)
        def _(n):
            cols = columns(n)
            both = pick0 + pick1
            gt[:, cols] = jnp.dot(both, retb[:, cols], preferred_element_type=F32).astype(BF16)

    back_at = 6
    out_at = 3 * (nz - 3) + 3

    @pl.loop(3, 3 * (nz - 1))
    def _(k):
        @pl.when(k == back_at)
        def _():
            input_back()

        @pl.when(k == out_at)
        def _():
            combine_out()

        scatter_step(lax.rem(k + 2, 3), k // 3 + 1)

    combine_back()
    for w, out in ((DOWN, od), (GATE, og), (UP, ou)):
        scatter_step(w, nz, out=out)

    @pl.loop(0, nz - 1)
    def _(s):
        for w in (GATE, UP, DOWN):
            for h in (0, 1):
                gather_copy(w, h, s).wait_send()
                scatter_copy(w, h, s + 1).wait_send()

    @pl.loop(1, ne)
    def _(o):
        for k, (src, dst) in enumerate(((outx, arrx), (outg, arrg), (prod, ret), (back, retb))):
            exchange(src, dst, k, o).wait_send()


def on_device(tokens, expert_ids, slot_index, routing_gates, grad_out, w_gate, w_up, w_down):
    tok_dev, top_k = expert_ids.shape
    width = tokens.shape[1]
    _, shard, hidden_units = w_gate.shape
    nz, ne = lax.axis_size("dp"), lax.axis_size("expert")
    cap = 2 * tok_dev * top_k // ne
    rows = ne * cap
    nc, nx = (2, 4) if ne % 8 == 0 else (1, ne)
    target = expert_ids * cap + slot_index
    vmem = pl.BlockSpec(memory_space=pltpu.VMEM)
    held = pl.BlockSpec(memory_space=pl.ANY)
    wide = lambda *lead: pltpu.VMEM((*lead, width), BF16)
    grad_w = jax.ShapeDtypeStruct(w_gate.shape, BF16)
    dma = pltpu.SemaphoreType.DMA
    return pl.pallas_call(
        functools.partial(layer_kernel, nz, ne, nx, nc, cap),
        out_shape=(
            jax.ShapeDtypeStruct(tokens.shape, BF16),
            jax.ShapeDtypeStruct(tokens.shape, BF16),
            jax.ShapeDtypeStruct(routing_gates.shape, F32),
            grad_w, grad_w, grad_w,
        ),
        in_specs=[vmem] * 6 + [held] * 3,
        out_specs=[vmem] * 6,
        scratch_shapes=[
            pltpu.VMEM((3, width, hidden_units), BF16),
            wide(rows), wide(rows), wide(rows), wide(rows),
            pltpu.VMEM((3, rows, hidden_units), F32),
            pltpu.VMEM((3, rows, hidden_units), BF16),
            wide(rows), wide(rows), wide(rows), wide(rows),
            pltpu.VMEM((2, width, rows), BF16),
            pltpu.VMEM((3, nz - 1, shard, hidden_units), BF16),
            pltpu.VMEM((3, nz - 1, shard, hidden_units), BF16),
            pltpu.VMEM((rows, tok_dev), BF16),
            pltpu.VMEM((rows, 128), F32),
            dma((3,)),
            dma((3, 2, nz - 1)), dma((3, 2, nz - 1)), dma((3, 2, nz - 1)), dma((3, 2, nz - 1)),
            dma((4, ne)), dma((4, ne)),
        ],
        compiler_params=pltpu.CompilerParams(
            collective_id=0, has_side_effects=True, vmem_limit_bytes=67043328
        ),
    )(
        target.T, routing_gates.T, target, routing_gates, tokens, grad_out, w_gate, w_up, w_down
    )


def solution(mesh):
    row = P(("dp", "expert"), None)
    weight = P("expert", "dp", None)
    return jax.shard_map(
        on_device,
        mesh=mesh,
        in_specs=(row,) * 5 + (weight,) * 3,
        out_specs=(row,) * 3 + (weight,) * 3,
        check_vma=False,
    )
```

time: 313 us -> 209 us (0.67)
  Pallas kernels: 0 us -> 196 us
  waiting for transfers between devices: 159 us -> 0 us
  matrix products: 47 us -> 0 us
  blocking collectives: 34.6 us -> 0 us
  starting transfers between devices: 20.4 us -> 0 us
  local copies, waits for them, and re-layouts: 24.8 us -> 9.78 us
  between operations: 14.3 us -> 0.66 us
  other arithmetic: 12.5 us -> 0.68 us
    pallas_call x0 -> x1, Pallas kernels: none -> 196 us  [on_device(): pl.pallas_call(functools.partial(layer_kernel, nz, ne, nx, nc, cap), out_...]
    all_to_all x3 -> x0, waiting for transfers between devices: 67.3 us -> none  [the longest x1 24 us: on_device(): lax.all_to_all(input_back.reshape(experts, capacity, model_width), 'exper...]
    dot_general x10 -> x0, matrix products: 47 us -> none  [the longest x3 15 us: partial_term(): lax.dot_general(left_rows, right_rows, (((0,), (0,)), ((), ())), preferre...]
    all_gather x3 -> x0, waiting for transfers between devices: 46.9 us -> none  [the longest x1 40 us: on_device(): lax.all_gather(w_gate, 'dp', axis=1, tiled=True)]
    reduce_scatter x3 -> x0, waiting for transfers between devices: 42.2 us -> none  [the longest x1 42.2 us: on_device(): lax.psum_scatter(partial_term(flat_grad, hidden).astype(jnp.bfloat16), 'd...]
    all_to_all x1 -> x0, blocking collectives: 34.6 us -> none  [on_device(): lax.all_to_all(grad_outbound, 'expert', split_axis=0, concat_axis=0, tile...]
    all_to_all x3 -> x0, starting transfers between devices: 20 us -> none  [the longest x1 7.43 us: on_device(): lax.all_to_all(produced.reshape(experts, slot_count, model_width), 'exper...]
    gather x4 -> x0, local copies, waits for them, and re-layouts: 13.2 us -> none  [the longest x1 4.25 us: on_device(): input_return.reshape(-1, model_width)[target]]
  transfers between devices with their start and end apart: 9 -> 0, of which waited for: 6 -> 0; matrix products, arithmetic and copies ran while one was open for 23% -> 0% of each run, Pallas kernels for 0% -> 0%
where the time goes in v1:
time: 209 us; the launch traced here: 207 us
  Pallas kernels  196 us (94%)
  local copies, waits for them, and re-layouts  9.78 us (5%)
    pallas_call x1, Pallas kernels, on_device(): pl.pallas_call(functools.partial(layer_kernel, nz, ne, nx, nc, cap), out_...  196 us
    unnamed x20, local copies, waits for them, and re-layouts  7.56 us

profile of v1, /device:TPU:2, one launch (start us, length us, event | category | flops | bytes accessed | tf_op | source)
XLA Modules:
  0.0 207.4 jit_solution(13777591429876458955)
XLA Ops:
  0.6 0.0 copy-start.6
  0.6 0.7 copy-done.6
  1.3 0.7 multiply_add_fusion
  2.0 0.0 copy-start.4
  2.0 0.0 copy-start.5
  2.0 0.7 copy.20.tgt_s
  2.7 0.0 copy-done.4
  2.7 0.0 copy-done.5
  2.7 0.7 copy.21.gate_s
  3.5 196.2 %shard_map.127 = (bf16[128,2048]{1,0:T(8,128)(2,1)}, bf16[128,2048]{1,0:T(8,128)(2,1)}, f32[128,2]{1,0:T(8,128)}, bf16[1,256,768]{2,1,0:T(8,128)(2,1)}, bf16[1,2...) custom-call(s32[2,128]{1,0:T(2,128)} %bitcast.2, f32[2,128]{1,0:T(2,128)} %bitcast.3, s32[128,2]{1,0:T(8,128)} %copy.20.tgt_s, ...), custom_call_target="tpu_custom_call" | custom-call | tf_op jit(solution)/shard_map/pallas_call | solution.py:360
  199.7 1.5 copy.22
  201.2 0.0 copy-start
  201.2 1.9 copy.28
  203.2 0.0 copy-done
  203.2 0.0 copy-start.3
  203.2 0.8 copy.29
  204.0 0.4 copy-done.3
  204.3 0.0 copy-start.2
  204.3 0.7 copy.30
  205.1 0.4 copy-done.2
  205.5 0.0 copy-start.1
  205.5 0.7 copy.31
  206.2 0.4 copy-done.1
  206.6 0.7 copy.32
Async XLA Ops:
  0.6 0.7 copy-start.6
  2.0 0.7 copy-start.4
  2.0 0.7 copy-start.5
  201.2 1.9 copy-start
  203.2 1.2 copy-start.3
  204.3 1.1 copy-start.2
  205.5 1.1 copy-start.1

commit v2 on v1

--- a/solution.py
+++ b/solution.py
@@ -12,20 +12,21 @@
 BF16 = jnp.bfloat16
 GATE, UP, DOWN = 0, 1, 2
 WIDE = 256
+LIMIT = 59 << 20
 
 
 def layer_kernel(
     nz, ne, nx, nc, cap,
-    tgt_l, gate_l, tgt_s, gate_s, tok, gout, wg, wu, wd,
+    ids, places, gate_l, tok_in, gout_in, wg, wu, wd,
     lo, gt, gg, og, ou, od,
-    wfull, outx, outg, arrx, arrg, pre, act, prod, back, ret, retb, xt, rsr, rss, onehot, slot_gate,
-    own_sem, ag_send, ag_recv, rs_send, rs_recv, a2a_send, a2a_recv,
+    wfull, outx, outg, arrx, arrg, pre, act, prod, back, ret, retb, xt, rsr, rss, onehot, slot_gate, term, tok, gout,
+    own_sem, row_sem, ag_send, ag_recv, rs_send, rs_recv, a2a_send, a2a_recv,
 ):
     z = lax.axis_index("dp")
     me = lax.axis_index("expert")
     right, left = lax.rem(z + 1, nz), lax.rem(z + nz - 1, nz)
     peers = (right, left)
-    width = tok.shape[1]
+    tok_dev, width = tok.shape
     hidden_units = wg.shape[2]
     shard = wg.shape[1]
     half = shard // 2
@@ -39,6 +40,10 @@
     ]
     for copy in own_copies:
         copy.start()
+    row_copies = [
+        pltpu.make_async_copy(ref, to, row_sem.at[k])
+        for k, (ref, to) in enumerate(((tok_in, tok), (gout_in, gout)))
+    ]
 
     def partner(o, sign):
         oc, ox, oy = lax.rem(o, nc), lax.rem(o // nc, nx), o // (nc * nx)
@@ -57,22 +62,11 @@
     def _(o):
         pl.semaphore_signal(barrier, inc=1, device_id={"expert": partner(o, 1)}, device_id_type=MESH)
 
-    slot = lax.broadcasted_iota(jnp.int32, onehot.shape, 0)
-    hit0, hit1 = slot == tgt_l[0:1, :], slot == tgt_l[1:2, :]
-    onehot[...] = jnp.where(hit0 | hit1, 1.0, 0.0).astype(BF16)
-    gates = jnp.where(hit0, gate_l[0:1, :], 0.0) + jnp.where(hit1, gate_l[1:2, :], 0.0)
-    slot_gate[...] = jnp.broadcast_to(jnp.sum(gates, axis=1, keepdims=True), slot_gate.shape)
-
     def columns(n, size=WIDE):
         return pl.ds(pl.multiple_of(n * size, size), size)
 
     def block(e):
         return pl.ds(pl.multiple_of(e * cap, cap), cap)
-
-    @pl.loop(0, width // WIDE)
-    def _(n):
-        cols = columns(n)
-        outx[:, cols] = jnp.dot(onehot[...], tok[:, cols], preferred_element_type=F32).astype(BF16)
 
     def piece(w, src, h):
         start = pl.multiple_of(lax.rem(src + 2 * nz, nz) * shard + h * half, half)
@@ -109,13 +103,29 @@
         def _(o):
             exchange(src, dst, k, o, arriving=True).wait_recv()
 
+    for copy in row_copies:
+        copy.start()
     for copy in own_copies:
         copy.wait()
     pl.semaphore_wait(barrier, ne + 1)
     for w in (GATE, UP, DOWN):
         for h in (0, 1):
             gather_copy(w, h, 0).start()
-    send_rows(outx, arrx, 0)
+
+    slot = lax.broadcasted_iota(jnp.int32, onehot.shape, 0)
+    tgt_l = ids[...] * cap + places[...]
+    hit0, hit1 = slot == tgt_l[0:1, :], slot == tgt_l[1:2, :]
+    onehot[...] = jnp.where(hit0 | hit1, 1.0, 0.0).astype(BF16)
+    gates = jnp.where(hit0, gate_l[0:1, :], 0.0) + jnp.where(hit1, gate_l[1:2, :], 0.0)
+    slot_gate[...] = jnp.broadcast_to(jnp.sum(gates, axis=1, keepdims=True), slot_gate.shape)
+
+    for copy in row_copies:
+        copy.wait()
+
+    @pl.loop(0, width // WIDE)
+    def _(n):
+        cols = columns(n)
+        outx[:, cols] = jnp.dot(onehot[...], tok[:, cols], preferred_element_type=F32).astype(BF16)
 
     @pl.loop(0, width // WIDE)
     def _(n):
@@ -124,6 +134,7 @@
         outg[:, cols] = (picked * slot_gate[:, 0:1]).astype(BF16)
 
     pre[...] = jnp.zeros_like(pre)
+    send_rows(outx, arrx, 0)
     send_rows(outg, arrg, 1)
 
     def halves(j):
@@ -205,29 +216,34 @@
 
     def scatter_step(w, i, first=False, out=None):
         a, b = halves(i)
+        k = w // 2
+        lhs = jnp.concatenate([xt[k, a, :], xt[k, b, :]], axis=0)
+        spans = [slice(n * WIDE, (n + 1) * WIDE) for n in range(hidden_units // WIDE)]
+        for cols in spans:
+            own_term = jnp.dot(lhs, act[w, :, cols], preferred_element_type=F32)
+            if first:
+                rss[w, i - 1, :, cols] = own_term.astype(BF16)
+            else:
+                term[:, cols] = own_term
         if not first:
             for h in (0, 1):
                 scatter_copy(w, h, i - 1).wait_recv()
-        k = w // 2
-        lhs = jnp.concatenate([xt[k, a, :], xt[k, b, :]], axis=0)
-        for n in range(hidden_units // WIDE):
-            cols = slice(n * WIDE, (n + 1) * WIDE)
-            term = jnp.dot(lhs, act[w, :, cols], preferred_element_type=F32)
-            if not first:
-                term = term + rsr[w, i - 2, :, cols].astype(F32)
-            if out is None:
-                rss[w, i - 1, :, cols] = term.astype(BF16)
-            else:
-                out[0, :, cols] = term.astype(BF16)
+            for cols in spans:
+                total = (term[:, cols] + rsr[w, i - 2, :, cols].astype(F32)).astype(BF16)
+                if out is None:
+                    rss[w, i - 1, :, cols] = total
+                else:
+                    out[0, :, cols] = total
         if out is None:
             for h in (0, 1):
                 scatter_copy(w, h, i).start()
 
     for h in (0, 1):
         gather_copy(GATE, h, last, arriving=True).wait_recv()
+    accumulate(GATE, arrx, nz - 1)
     for h in (0, 1):
         gather_copy(UP, h, last, arriving=True).wait_recv()
-    accumulate_gate_up(nz - 1, nz)
+    accumulate(UP, arrx, nz - 1)
 
     @pl.loop(0, rows // tile)
     def _(r):
@@ -272,25 +288,28 @@
 
         send_rows(back, retb, 3)
 
-    tok_dev = tok.shape[0]
     slots = lax.broadcasted_iota(jnp.int32, (tok_dev, rows), 1)
 
+    def column(row):
+        return jnp.broadcast_to(row, (tok_dev, tok_dev)).T[:, 0:1]
+
     def picks():
-        return (
-            jnp.where(slots == tgt_s[:, 0:1], 1.0, 0.0).astype(BF16),
-            jnp.where(slots == tgt_s[:, 1:2], 1.0, 0.0).astype(BF16),
-        )
+        tgt = ids[...] * cap + places[...]
+        return [
+            jnp.where(slots == column(tgt[k : k + 1, :]), 1.0, 0.0).astype(BF16) for k in (0, 1)
+        ]
 
     def combine_out():
         await_rows(prod, ret, 2)
         pick0, pick1 = picks()
+        gate0, gate1 = column(gate_l[0:1, :]), column(gate_l[1:2, :])
         zero = jnp.zeros((tok_dev, 1), F32)
 
         def step(n, sums):
             cols = columns(n)
             r0 = jnp.dot(pick0, ret[:, cols], preferred_element_type=F32)
             r1 = jnp.dot(pick1, ret[:, cols], preferred_element_type=F32)
-            lo[:, cols] = (gate_s[:, 0:1] * r0 + gate_s[:, 1:2] * r1).astype(BF16)
+            lo[:, cols] = (gate0 * r0 + gate1 * r1).astype(BF16)
             cot = gout[:, cols].astype(F32)
             return (
                 sums[0] + jnp.sum(r0 * cot, axis=1, keepdims=True),
@@ -298,8 +317,8 @@
             )
 
         d0, d1 = lax.fori_loop(0, width // WIDE, step, (zero, zero))
-        which = lax.broadcasted_iota(jnp.int32, gg.shape, 1)
-        gg[...] = jnp.where(which == 0, d0, d1)
+        for k, d in enumerate((d0, d1)):
+            gg[k : k + 1, :] = jnp.broadcast_to(d, (tok_dev, tok_dev)).T[0:1, :]
 
     def combine_back():
         await_rows(back, retb, 3)
@@ -341,6 +360,18 @@
     def _(o):
         for k, (src, dst) in enumerate(((outx, arrx), (outg, arrg), (prod, ret), (back, retb))):
             exchange(src, dst, k, o).wait_send()
+
+
+def write_kernel(*refs):
+    sems = refs[-1]
+    count = (len(refs) - 1) // 2
+    copies = [
+        pltpu.make_async_copy(refs[k], refs[count + k], sems.at[k]) for k in range(count)
+    ]
+    for copy in copies:
+        copy.start()
+    for copy in copies:
+        copy.wait()
 
 
 def on_device(tokens, expert_ids, slot_index, routing_gates, grad_out, w_gate, w_up, w_down):
@@ -351,21 +382,22 @@
     cap = 2 * tok_dev * top_k // ne
     rows = ne * cap
     nc, nx = (2, 4) if ne % 8 == 0 else (1, ne)
-    target = expert_ids * cap + slot_index
     vmem = pl.BlockSpec(memory_space=pltpu.VMEM)
     held = pl.BlockSpec(memory_space=pl.ANY)
     wide = lambda *lead: pltpu.VMEM((*lead, width), BF16)
-    grad_w = jax.ShapeDtypeStruct(w_gate.shape, BF16)
     dma = pltpu.SemaphoreType.DMA
-    return pl.pallas_call(
+    outs = (
+        (tokens.shape, BF16),
+        (tokens.shape, BF16),
+        ((top_k, tok_dev), F32),
+        (w_gate.shape, BF16),
+        (w_gate.shape, BF16),
+        (w_gate.shape, BF16),
+    )
+    results = pl.pallas_call(
         functools.partial(layer_kernel, nz, ne, nx, nc, cap),
-        out_shape=(
-            jax.ShapeDtypeStruct(tokens.shape, BF16),
-            jax.ShapeDtypeStruct(tokens.shape, BF16),
-            jax.ShapeDtypeStruct(routing_gates.shape, F32),
-            grad_w, grad_w, grad_w,
-        ),
-        in_specs=[vmem] * 6 + [held] * 3,
+        out_shape=tuple(pltpu.VMEM(*out) for out in outs),
+        in_specs=[vmem] * 3 + [held] * 5,
         out_specs=[vmem] * 6,
         scratch_shapes=[
             pltpu.VMEM((3, width, hidden_units), BF16),
@@ -378,16 +410,25 @@
             pltpu.VMEM((3, nz - 1, shard, hidden_units), BF16),
             pltpu.VMEM((rows, tok_dev), BF16),
             pltpu.VMEM((rows, 128), F32),
-            dma((3,)),
+            pltpu.VMEM((shard, hidden_units), F32),
+            wide(tok_dev), wide(tok_dev),
+            dma((3,)), dma((2,)),
             dma((3, 2, nz - 1)), dma((3, 2, nz - 1)), dma((3, 2, nz - 1)), dma((3, 2, nz - 1)),
             dma((4, ne)), dma((4, ne)),
         ],
         compiler_params=pltpu.CompilerParams(
-            collective_id=0, has_side_effects=True, vmem_limit_bytes=67043328
+            collective_id=0, has_side_effects=True, vmem_limit_bytes=LIMIT
         ),
-    )(
-        target.T, routing_gates.T, target, routing_gates, tokens, grad_out, w_gate, w_up, w_down
-    )
+    )(expert_ids.T, slot_index.T, routing_gates.T, tokens, grad_out, w_gate, w_up, w_down)
+    layer_out, grad_tokens, grad_gates, *grads = pl.pallas_call(
+        write_kernel,
+        out_shape=tuple(jax.ShapeDtypeStruct(*out) for out in outs),
+        in_specs=[vmem] * 6,
+        out_specs=[held] * 6,
+        scratch_shapes=[dma((6,))],
+        compiler_params=pltpu.CompilerParams(vmem_limit_bytes=4 << 20),
+    )(*results)
+    return layer_out, grad_tokens, grad_gates.T, *grads
 
 
 def solution(mesh):

time: 209 us -> 198 us (0.947)
  local copies, waits for them, and re-layouts: 9.78 us -> 0 us
    unnamed x20 -> x0, local copies, waits for them, and re-layouts: 7.56 us -> none
    pallas_call x1, Pallas kernels: 196 us -> 194 us  [on_device(): pl.pallas_call(functools.partial(layer_kernel, nz, ne, nx, nc, cap), out_...]
where the time goes in v2:
time: 198 us; the launch traced here: 196 us
  Pallas kernels  195 us (98%)
    pallas_call x1, Pallas kernels, on_device(): pl.pallas_call(functools.partial(layer_kernel, nz, ne, nx, nc, cap), out_...  194 us

profile of v2, /device:TPU:2, one launch (start us, length us, event | category | flops | bytes accessed | tf_op | source)
XLA Modules:
  0.0 196.0 jit_solution(1919303516896555962)
XLA Ops:
  0.6 193.9 %shard_map.127 = (bf16[128,2048]{1,0:T(8,128)(2,1)S(1)}, bf16[128,2048]{1,0:T(8,128)(2,1)S(1)}, f32[2,128]{1,0:T(2,128)S(1)}, bf16[1,256,768]{2,1,0:T(8,128)(2,1...) custom-call(s32[2,128]{1,0:T(2,128)} %bitcast.4, s32[2,128]{1,0:T(2,128)} %bitcast.5, ...), custom_call_target="tpu_custom_call" | custom-call | tf_op jit(solution)/shard_map/pallas_call | solution.py:397
  194.6 1.4 shard_map.128

commit v3 on v2

--- a/solution.py
+++ b/solution.py
@@ -20,7 +20,7 @@
     ids, places, gate_l, tok_in, gout_in, wg, wu, wd,
     lo, gt, gg, og, ou, od,
     wfull, outx, outg, arrx, arrg, pre, act, prod, back, ret, retb, xt, rsr, rss, onehot, slot_gate, term, tok, gout,
-    own_sem, row_sem, ag_send, ag_recv, rs_send, rs_recv, a2a_send, a2a_recv,
+    near_sem, own_sem, row_sem, ag_send, ag_recv, rs_send, rs_recv, a2a_send, a2a_recv,
 ):
     z = lax.axis_index("dp")
     me = lax.axis_index("expert")
@@ -58,9 +58,19 @@
     for peer in peers:
         pl.semaphore_signal(barrier, inc=1, device_id={"dp": peer}, device_id_type=MESH)
 
-    @pl.loop(1, ne)
-    def _(o):
-        pl.semaphore_signal(barrier, inc=1, device_id={"expert": partner(o, 1)}, device_id_type=MESH)
+    ny = ne // (nc * nx)
+    near, reach = [], 0
+    for size, stride in ((nc, 1), (nx, nc), (ny, nc * nx)):
+        here = lax.rem(me // stride, size)
+        for step in sorted({1, size - 1} - {0}):
+            near.append(me + (lax.rem(here + step, size) - here) * stride)
+        reach += size // 2
+
+    def greet(sem):
+        for e in near:
+            pl.semaphore_signal(sem, inc=1, device_id={"expert": e}, device_id_type=MESH)
+
+    greet(barrier)
 
     def columns(n, size=WIDE):
         return pl.ds(pl.multiple_of(n * size, size), size)
@@ -107,10 +117,14 @@
         copy.start()
     for copy in own_copies:
         copy.wait()
-    pl.semaphore_wait(barrier, ne + 1)
+    pl.semaphore_wait(barrier, len(near) + 2)
     for w in (GATE, UP, DOWN):
         for h in (0, 1):
             gather_copy(w, h, 0).start()
+
+    for r in range(reach - 1):
+        greet(near_sem.at[r])
+        pl.semaphore_wait(near_sem.at[r], len(near))
 
     slot = lax.broadcasted_iota(jnp.int32, onehot.shape, 0)
     tgt_l = ids[...] * cap + places[...]
@@ -346,20 +360,31 @@
         scatter_step(lax.rem(k + 2, 3), k // 3 + 1)
 
     combine_back()
-    for w, out in ((DOWN, od), (GATE, og), (UP, ou)):
-        scatter_step(w, nz, out=out)
-
-    @pl.loop(0, nz - 1)
-    def _(s):
-        for w in (GATE, UP, DOWN):
-            for h in (0, 1):
-                gather_copy(w, h, s).wait_send()
-                scatter_copy(w, h, s + 1).wait_send()
 
     @pl.loop(1, ne)
     def _(o):
         for k, (src, dst) in enumerate(((outx, arrx), (outg, arrg), (prod, ret), (back, retb))):
             exchange(src, dst, k, o).wait_send()
+
+    def sent(s, gathered):
+        for w in (GATE, UP, DOWN):
+            for h in (0, 1):
+                if gathered:
+                    gather_copy(w, h, s).wait_send()
+                else:
+                    scatter_copy(w, h, s + 1).wait_send()
+
+    @pl.loop(0, nz - 1)
+    def _(s):
+        sent(s, True)
+
+    @pl.loop(0, nz - 2)
+    def _(s):
+        sent(s, False)
+
+    for w, out in ((DOWN, od), (GATE, og), (UP, ou)):
+        scatter_step(w, nz, out=out)
+    sent(nz - 2, False)
 
 
 def write_kernel(*refs):
@@ -412,6 +437,7 @@
             pltpu.VMEM((rows, 128), F32),
             pltpu.VMEM((shard, hidden_units), F32),
             wide(tok_dev), wide(tok_dev),
+            pltpu.SemaphoreType.REGULAR((8,)),
             dma((3,)), dma((2,)),
             dma((3, 2, nz - 1)), dma((3, 2, nz - 1)), dma((3, 2, nz - 1)), dma((3, 2, nz - 1)),
             dma((4, ne)), dma((4, ne)),

time: 198 us -> 193 us (0.975); the launches traced: 196 us -> 193 us
  Pallas kernels: 195 us -> 192 us
    pallas_call x1, Pallas kernels: 194 us -> 191 us  [on_device(): pl.pallas_call(functools.partial(layer_kernel, nz, ne, nx, nc, cap), out_...]
where the time goes in v3:
time: 193 us
  Pallas kernels  192 us (99%)
    pallas_call x1, Pallas kernels, on_device(): pl.pallas_call(functools.partial(layer_kernel, nz, ne, nx, nc, cap), out_...  191 us

profile of v3, /device:TPU:2, one launch (start us, length us, event | category | flops | bytes accessed | tf_op | source)
XLA Modules:
  0.0 193.0 jit_solution(9715260376866203804)
XLA Ops:
  0.6 190.9 %shard_map.127 = (bf16[128,2048]{1,0:T(8,128)(2,1)S(1)}, bf16[128,2048]{1,0:T(8,128)(2,1)S(1)}, f32[2,128]{1,0:T(2,128)S(1)}, bf16[1,256,768]{2,1,0:T(8,128)(2,1...) custom-call(s32[2,128]{1,0:T(2,128)} %bitcast.4, s32[2,128]{1,0:T(2,128)} %bitcast.5, ...), custom_call_target="tpu_custom_call" | custom-call | tf_op jit(solution)/shard_map/pallas_call | solution.py:422
  191.6 1.4 shard_map.128

commit v4 on v3

--- a/solution.py
+++ b/solution.py
@@ -17,9 +17,9 @@
 
 def layer_kernel(
     nz, ne, nx, nc, cap,
-    ids, places, gate_l, tok_in, gout_in, wg, wu, wd,
+    ids_in, places_in, gate_in, tok_in, gout_in, wg, wu, wd,
     lo, gt, gg, og, ou, od,
-    wfull, outx, outg, arrx, arrg, pre, act, prod, back, ret, retb, xt, rsr, rss, onehot, slot_gate, term, tok, gout,
+    wfull, outx, outg, arrx, arrg, pre, act, prod, back, ret, retb, xt, rsr, rss, onehot, slot_gate, term, tok, gout, ids, places, gate_l,
     near_sem, own_sem, row_sem, ag_send, ag_recv, rs_send, rs_recv, a2a_send, a2a_recv,
 ):
     z = lax.axis_index("dp")
@@ -38,11 +38,14 @@
         pltpu.make_async_copy(ref.at[0], wfull.at[w, own, :], own_sem.at[w])
         for w, ref in ((GATE, wg), (UP, wu), (DOWN, wd))
     ]
-    for copy in own_copies:
-        copy.start()
     row_copies = [
         pltpu.make_async_copy(ref, to, row_sem.at[k])
-        for k, (ref, to) in enumerate(((tok_in, tok), (gout_in, gout)))
+        for k, (ref, to) in enumerate(
+            (
+                (ids_in, ids), (places_in, places), (gate_in, gate_l),
+                (tok_in, tok), (gout_in, gout),
+            )
+        )
     ]
 
     def partner(o, sign):
@@ -82,11 +85,11 @@
         start = pl.multiple_of(lax.rem(src + 2 * nz, nz) * shard + h * half, half)
         return wfull.at[w, pl.ds(start, half), :]
 
-    def gather_copy(w, h, s, arriving=False):
+    def gather_copy(w, h, s, arriving=False, source=None):
         hop = s + 1 if arriving else s
         ref = piece(w, z - hop if h == 0 else z + hop, h)
         return pltpu.make_async_remote_copy(
-            src_ref=ref, dst_ref=ref,
+            src_ref=ref if source is None else source, dst_ref=ref,
             send_sem=ag_send.at[w, h, s], recv_sem=ag_recv.at[w, h, s],
             device_id={"dp": peers[h]}, device_id_type=MESH,
         )
@@ -113,19 +116,19 @@
         def _(o):
             exchange(src, dst, k, o, arriving=True).wait_recv()
 
-    for copy in row_copies:
+    pl.semaphore_wait(barrier, len(near) + 2)
+    for w, ref in ((GATE, wg), (UP, wu), (DOWN, wd)):
+        for h in (0, 1):
+            gather_copy(w, h, 0, source=ref.at[0, pl.ds(h * half, half), :]).start()
+    for copy in row_copies + own_copies:
         copy.start()
-    for copy in own_copies:
-        copy.wait()
-    pl.semaphore_wait(barrier, len(near) + 2)
-    for w in (GATE, UP, DOWN):
-        for h in (0, 1):
-            gather_copy(w, h, 0).start()
 
     for r in range(reach - 1):
         greet(near_sem.at[r])
         pl.semaphore_wait(near_sem.at[r], len(near))
 
+    for copy in row_copies + own_copies:
+        copy.wait()
     slot = lax.broadcasted_iota(jnp.int32, onehot.shape, 0)
     tgt_l = ids[...] * cap + places[...]
     hit0, hit1 = slot == tgt_l[0:1, :], slot == tgt_l[1:2, :]
@@ -133,8 +136,6 @@
     gates = jnp.where(hit0, gate_l[0:1, :], 0.0) + jnp.where(hit1, gate_l[1:2, :], 0.0)
     slot_gate[...] = jnp.broadcast_to(jnp.sum(gates, axis=1, keepdims=True), slot_gate.shape)
 
-    for copy in row_copies:
-        copy.wait()
 
     @pl.loop(0, width // WIDE)
     def _(n):
@@ -422,7 +423,7 @@
     results = pl.pallas_call(
         functools.partial(layer_kernel, nz, ne, nx, nc, cap),
         out_shape=tuple(pltpu.VMEM(*out) for out in outs),
-        in_specs=[vmem] * 3 + [held] * 5,
+        in_specs=[held] * 8,
         out_specs=[vmem] * 6,
         scratch_shapes=[
             pltpu.VMEM((3, width, hidden_units), BF16),
@@ -437,8 +438,10 @@
             pltpu.VMEM((rows, 128), F32),
             pltpu.VMEM((shard, hidden_units), F32),
             wide(tok_dev), wide(tok_dev),
+            pltpu.VMEM((top_k, tok_dev), jnp.int32), pltpu.VMEM((top_k, tok_dev), jnp.int32),
+            pltpu.VMEM((top_k, tok_dev), F32),
             pltpu.SemaphoreType.REGULAR((8,)),
-            dma((3,)), dma((2,)),
+            dma((3,)), dma((5,)),
             dma((3, 2, nz - 1)), dma((3, 2, nz - 1)), dma((3, 2, nz - 1)), dma((3, 2, nz - 1)),
             dma((4, ne)), dma((4, ne)),
         ],

time: 193 us -> 193 us (level)
  no operation moved by 1% of the time
where the time goes in v4:
time: 193 us
  Pallas kernels  192 us (99%)
    pallas_call x1, Pallas kernels, on_device(): pl.pallas_call(functools.partial(layer_kernel, nz, ne, nx, nc, cap), out_...  191 us

profile of v4, /device:TPU:2, one launch (start us, length us, event | category | flops | bytes accessed | tf_op | source)
XLA Modules:
  0.0 192.6 jit_solution(6041214425807428347)
XLA Ops:
  0.6 190.5 %shard_map.127 = (bf16[128,2048]{1,0:T(8,128)(2,1)S(1)}, bf16[128,2048]{1,0:T(8,128)(2,1)S(1)}, f32[2,128]{1,0:T(2,128)S(1)}, bf16[1,256,768]{2,1,0:T(8,128)(2,1...) custom-call(s32[2,128]{1,0:T(2,128)} %bitcast.4, s32[2,128]{1,0:T(2,128)} %bitcast.5, ...), custom_call_target="tpu_custom_call" | custom-call | tf_op jit(solution)/shard_map/pallas_call | solution.py:423
  191.2 1.4 shard_map.128

commit v5 on v4

--- a/solution.py
+++ b/solution.py
@@ -183,7 +183,7 @@
             cols = columns(n)
             xt[k, cols, :] = src[:, cols].T
 
-    x_step, g_step = min(3, last - 1), min(5, last - 1)
+    x_step, g_step = min(4, last - 1), min(5, last - 1)
 
     @pl.loop(0, last)
     def _(s):
@@ -243,13 +243,16 @@
         if not first:
             for h in (0, 1):
                 scatter_copy(w, h, i - 1).wait_recv()
-            for cols in spans:
-                total = (term[:, cols] + rsr[w, i - 2, :, cols].astype(F32)).astype(BF16)
+                side = slice(h * half, (h + 1) * half)
+                for cols in spans:
+                    total = term[side, cols] + rsr[w, i - 2, side, cols].astype(F32)
+                    if out is None:
+                        rss[w, i - 1, side, cols] = total.astype(BF16)
+                    else:
+                        out[0, side, cols] = total.astype(BF16)
                 if out is None:
-                    rss[w, i - 1, :, cols] = total
-                else:
-                    out[0, :, cols] = total
-        if out is None:
+                    scatter_copy(w, h, i).start()
+        else:
             for h in (0, 1):
                 scatter_copy(w, h, i).start()
 
@@ -345,7 +348,7 @@
             both = pick0 + pick1
             gt[:, cols] = jnp.dot(both, retb[:, cols], preferred_element_type=F32).astype(BF16)
 
-    back_at = 6
+    back_at = 9
     out_at = 3 * (nz - 3) + 3
 
     @pl.loop(3, 3 * (nz - 1))

time: 193 us -> 193 us (level)
  no operation moved by 1% of the time
where the time goes in v5:
time: 193 us
  Pallas kernels  192 us (99%)
    pallas_call x1, Pallas kernels, on_device(): pl.pallas_call(functools.partial(layer_kernel, nz, ne, nx, nc, cap), out_...  191 us

profile of v5, /device:TPU:2, one launch (start us, length us, event | category | flops | bytes accessed | tf_op | source)
XLA Modules:
  0.0 192.6 jit_solution(14010401951916858936)
XLA Ops:
  0.6 190.5 %shard_map.127 = (bf16[128,2048]{1,0:T(8,128)(2,1)S(1)}, bf16[128,2048]{1,0:T(8,128)(2,1)S(1)}, f32[2,128]{1,0:T(2,128)S(1)}, bf16[1,256,768]{2,1,0:T(8,128)(2,1...) custom-call(s32[2,128]{1,0:T(2,128)} %bitcast.4, s32[2,128]{1,0:T(2,128)} %bitcast.5, ...), custom_call_target="tpu_custom_call" | custom-call | tf_op jit(solution)/shard_map/pallas_call | solution.py:426
  191.2 1.4 shard_map.128
